TPU v7x, 32 devices: a whole 2x2x4 slice. The times are simulated.
32 devices in a mesh: tm: 4 (over y, x), space: 8 (over z, core).
Axes of the slice: x: 2, y: 2, z: 4, core: 2. Of those that a mesh axis runs over, the one named last changes fastest.
Arguments:
- starts: float32 [4, 8192, 128], P('tm', 'space'), may hold values from -6 to 6
- volume_op: float32 [128, 128], replicated, may hold values from -0.1875 to 0.1875
- face_lifts: float32 [6, 128, 128], replicated, may hold values from -0.1875 to 0.1875
- neighbours: int32 [8192, 6], P('space'), may hold values from 0 to 8191, as said below
- orientation: int32 [8192, 6], P('space'), may hold values from 0 to 3
Outputs:
- updated: float32 [4, 8192, 128], P('tm', 'space')
Inputs may be any that keep to these rules, and one draw needn't show every extreme that they name: neighbours[e, f] lies at most 128 elements from e in the periodic element order, that is it equals (e + k) mod 8192 with -128 <= k <= 128; both k = 128 and k = -128 occur.
All inputs are finite; a program needn't handle non-finite values.
Results may differ from a plain program's by a relative error of at most 0.0001.
Values sent between devices are 32-bit elements; how exact they have to be, the bound alone decides.
A program may use at most 64 MiB of HBM per device.

v0:
```python
import jax
import jax.numpy as jnp
from jax import lax
from jax.sharding import PartitionSpec as P

REACH = 128
STEPS = 4


FINE_DT = 0.25
COARSE_DT = 1.0


def padded(cells, sides, width):
    for axis, dim in sides:
        count = lax.axis_size(axis)
        head = lax.slice_in_dim(cells, 0, width, axis=dim)
        tail = lax.slice_in_dim(cells, cells.shape[dim] - width, cells.shape[dim], axis=dim)
        cells = jnp.concatenate(
            [
                lax.ppermute(tail, axis, [(i, (i + 1) % count) for i in range(count)]),
                cells,
                lax.ppermute(head, axis, [((i + 1) % count, i) for i in range(count)]),
            ],
            axis=dim,
        )
    return cells


def from_behind(block, axis, distance):
    devices = range(lax.axis_size(axis))
    route = [(i - distance, i) for i in devices if i - distance in devices]
    return lax.ppermute(block, axis, route)


def twist_rows(gathered, orient_ids):
    node_count = gathered.shape[-1]
    flipped = jnp.where((orient_ids % 2 == 1)[..., None], gathered[..., ::-1], gathered)
    return jnp.where(
        (orient_ids // 2 == 1)[..., None], jnp.roll(flipped, node_count // 2, axis=-1), flipped
    )


def operate(center, extended, places, orient_ids, volume_op, face_lifts):
    elem_count, node_count = center.shape
    faces = twist_rows(extended[places], orient_ids).reshape(elem_count, 6 * node_count)
    flux = jnp.dot(
        faces,
        face_lifts.reshape(6 * node_count, node_count),
        precision=lax.Precision.HIGHEST,
        preferred_element_type=jnp.float32,
    )
    inner = jnp.dot(
        center, volume_op, precision=lax.Precision.HIGHEST, preferred_element_type=jnp.float32
    )
    return inner + flux - center


def local_places(neighbour_ids, first_global, elem_total, shift_rows):
    row_count = neighbour_ids.shape[0]
    row_index = jnp.arange(row_count, dtype=jnp.int32)
    global_rows = first_global + row_index
    offsets = (neighbour_ids - global_rows[:, None] + REACH) % elem_total - REACH
    return row_index[:, None] + shift_rows + offsets


def per_device(starts, volume_op, face_lifts, neighbours, orientation):
    first_state = starts[0]
    elem_count = first_state.shape[0]
    elem_total = elem_count * lax.axis_size("space")
    first_row = lax.axis_index("space") * elem_count
    places = local_places(neighbours, first_row, elem_total, REACH)

    def coarse_apply(state):
        extended = padded(state, (("space", 0),), REACH)
        return state + COARSE_DT * operate(
            state, extended, places, orientation, volume_op, face_lifts
        )

    fine_state = first_state
    for step_idx in range(STEPS):
        extended = padded(fine_state, (("space", 0),), REACH)
        fine_state = fine_state + FINE_DT * operate(
            fine_state, extended, places, orientation, volume_op, face_lifts
        )
    slot_id = lax.axis_index("tm")
    coarse_here = coarse_apply(first_state)
    correction = jnp.where(slot_id == 0, fine_state, fine_state - coarse_here)

    def advance(loop_idx, result):
        arrived = from_behind(result, "tm", 1)
        return coarse_apply(arrived) + correction

    result = lax.fori_loop(0, lax.axis_size("tm") - 1, advance, correction)
    return result[None]


def solution(mesh):
    return jax.shard_map(
        per_device,
        mesh=mesh,
        in_specs=(P("tm", "space", None), P(), P(), P("space", None), P("space", None)),
        out_specs=P("tm", "space", None),
        check_vma=False,
    )
```

profile of v0, /device:TPU:4, one launch (start us, length us, event | category | flops | bytes accessed | tf_op | source)
XLA Modules:
  0.0 429.1 jit_solution(11519850679134375305)
XLA Ops:
  0.9 3.5 collective-permute-start.4
  8.4 21.1 %gather_fusion.1 = f32[6144,128]{1,0:T(8,128)} fusion(f32[1280,128]{1,0:T(8,128)S(1)} %pad_maximum_fusion.1, s32[6144]{0:T(1024)S(1)} %broadcast_clamp_fusion.1), kind=kCustom, calls=%fused_computation.1 | custom fusion | bytes 6316032 | tf_op jit(solution)/shard_map/gather | solution.py:46
  29.4 4.6 %reshape.103 = f32[1024,6,128]{2,1,0:T(8,128)} reshape(f32[6144,128]{1,0:T(8,128)} %gather_fusion.1) | data formatting | bytes 6291456 | tf_op jit(solution)/shard_map/gather | solution.py:46
  34.0 7.2 %rev.21 = f32[1024,6,128]{2,1,0:T(8,128)} reverse(f32[1024,6,128]{2,1,0:T(8,128)} %reshape.103), dimensions={2} | reverse | bytes 6291456 | tf_op jit(solution)/shard_map/rev | solution.py:38
  41.2 6.1 %broadcast_select_fusion.4 = f32[1024,6,128]{2,1,0:T(8,128)S(1)} fusion(f32[1024,6,128]{2,1,0:T(8,128)} %rev.21, f32[1024,6,128]{2,1,0:T(8,128)} %reshape.103, pred[1024,6]{1,0:T(8,128)(4,1)S(1)} %copy.30), kind=kLoop, calls=%fused_computation.42 | loop fusion | flops 786432 | bytes 9443328 | tf_op jit(solution)/shard_map/jit(_where)/select_n | solution.py:38
  48.7 3.3 maximum_select_fusion.1
  56.1 4.0 collective-permute-start.6
  62.1 21.1 %gather_fusion.2 = f32[6144,128]{1,0:T(8,128)} fusion(f32[1280,128]{1,0:T(8,128)S(1)} %pad_maximum_fusion.2, s32[6144]{0:T(1024)S(1)} %broadcast_clamp_fusion.1), kind=kCustom, calls=%fused_computation.2 | custom fusion | bytes 6316032 | tf_op jit(solution)/shard_map/gather | solution.py:46
  83.2 4.6 %reshape.111 = f32[1024,6,128]{2,1,0:T(8,128)} reshape(f32[6144,128]{1,0:T(8,128)} %gather_fusion.2) | data formatting | bytes 6291456 | tf_op jit(solution)/shard_map/gather | solution.py:46
  87.7 7.2 %rev.22 = f32[1024,6,128]{2,1,0:T(8,128)} reverse(f32[1024,6,128]{2,1,0:T(8,128)} %reshape.111), dimensions={2} | reverse | bytes 6291456 | tf_op jit(solution)/shard_map/rev | solution.py:38
  95.0 6.1 %broadcast_select_fusion.3 = f32[1024,6,128]{2,1,0:T(8,128)S(1)} fusion(f32[1024,6,128]{2,1,0:T(8,128)} %rev.22, f32[1024,6,128]{2,1,0:T(8,128)} %reshape.111, pred[1024,6]{1,0:T(8,128)(4,1)S(1)} %copy.30), kind=kLoop, calls=%fused_computation.41 | loop fusion | flops 786432 | bytes 9443328 | tf_op jit(solution)/shard_map/jit(_where)/select_n | solution.py:38
  102.4 3.3 maximum_select_fusion.2
  109.0 3.8 collective-permute-start.8
  114.8 21.1 %gather_fusion.3 = f32[6144,128]{1,0:T(8,128)} fusion(f32[1280,128]{1,0:T(8,128)S(1)} %pad_maximum_fusion.3, s32[6144]{0:T(1024)S(1)} %broadcast_clamp_fusion.1), kind=kCustom, calls=%fused_computation.3 | custom fusion | bytes 6316032 | tf_op jit(solution)/shard_map/gather | solution.py:46
  135.8 4.6 %reshape.119 = f32[1024,6,128]{2,1,0:T(8,128)} reshape(f32[6144,128]{1,0:T(8,128)} %gather_fusion.3) | data formatting | bytes 6291456 | tf_op jit(solution)/shard_map/gather | solution.py:46
  140.4 7.2 %rev.23 = f32[1024,6,128]{2,1,0:T(8,128)} reverse(f32[1024,6,128]{2,1,0:T(8,128)} %reshape.119), dimensions={2} | reverse | bytes 6291456 | tf_op jit(solution)/shard_map/rev | solution.py:38
  147.7 6.1 %broadcast_select_fusion.2 = f32[1024,6,128]{2,1,0:T(8,128)S(1)} fusion(f32[1024,6,128]{2,1,0:T(8,128)} %rev.23, f32[1024,6,128]{2,1,0:T(8,128)} %reshape.119, pred[1024,6]{1,0:T(8,128)(4,1)S(1)} %copy.30), kind=kLoop, calls=%fused_computation.40 | loop fusion | flops 786432 | bytes 9443328 | tf_op jit(solution)/shard_map/jit(_where)/select_n | solution.py:38
  155.1 3.3 maximum_select_fusion.3
  161.6 3.6 collective-permute-start.10
  168.3 2.6 collective-permute-done.9
  172.1 21.1 %gather_fusion.4 = f32[6144,128]{1,0:T(8,128)} fusion(f32[1280,128]{1,0:T(8,128)S(1)} %pad_maximum_fusion.4, s32[6144]{0:T(1024)S(1)} %broadcast_clamp_fusion.1), kind=kCustom, calls=%fused_computation.4 | custom fusion | bytes 6316032 | tf_op jit(solution)/shard_map/gather | solution.py:46
  193.1 4.6 %reshape.127 = f32[1024,6,128]{2,1,0:T(8,128)} reshape(f32[6144,128]{1,0:T(8,128)} %gather_fusion.4) | data formatting | bytes 6291456 | tf_op jit(solution)/shard_map/gather | solution.py:46
  197.7 7.2 %rev.24 = f32[1024,6,128]{2,1,0:T(8,128)} reverse(f32[1024,6,128]{2,1,0:T(8,128)} %reshape.127), dimensions={2} | reverse | bytes 6291456 | tf_op jit(solution)/shard_map/rev | solution.py:38
  204.9 6.1 %broadcast_select_fusion.1 = f32[1024,6,128]{2,1,0:T(8,128)S(1)} fusion(f32[1024,6,128]{2,1,0:T(8,128)} %rev.24, f32[1024,6,128]{2,1,0:T(8,128)} %reshape.127, pred[1024,6]{1,0:T(8,128)(4,1)S(1)} %copy.30), kind=kLoop, calls=%fused_computation.39 | loop fusion | flops 786432 | bytes 9443328 | tf_op jit(solution)/shard_map/jit(_where)/select_n | solution.py:38
  212.4 3.3 maximum_select_fusion.4
  220.0 208.8 %while.14 = (s32[]{:T(128)}, f32[1024,128]{1,0:T(8,128)}, f32[128,128]{1,0:T(8,128)S(1)}, s32[1024,6,1]{1,0,2:T(8,128)S(1)}, s32[1024,6]{1,0:T(8,128)S(1)}, /*in...) while((s32[]{:T(128)}, f32[1024,128]{1,0:T(8,128)}, ...), condition=%wide.region_1.2_spmd, body=%wide.region_0.1_spmd.sunk | while | flops 1412669440 | bytes 57114916 | solution.py:94
  220.2 3.4 collective-permute-start
  225.7 7.1 %collective-permute-done = f32[1024,128]{1,0:T(8,128)S(1)} collective-permute-done((f32[1024,128]{1,0:T(8,128)}, f32[1024,128]{1,0:T(8,128)S(1)}, u32[]{:S(2)}, u32[]{:S(2)}) %collective-permute-start) | collective-permute-done | bytes 524320 | tf_op jit(solution)/shard_map/while/body/eval_jaxpr/ppermute | solution.py:33
  237.2 3.7 collective-permute-done.2
  241.8 21.1 %gather_fusion = f32[6144,128]{1,0:T(8,128)} fusion(f32[1280,128]{1,0:T(8,128)S(1)} %pad_maximum_fusion.6, s32[6144]{0:T(1024)S(1)} %broadcast_clamp_fusion.3), kind=kCustom, calls=%fused_computation.clone.1 | custom fusion | bytes 6316032 | tf_op jit(solution)/shard_map/while/body/eval_jaxpr/gather | solution.py:46
  262.9 4.6 %reshape.155 = f32[1024,6,128]{2,1,0:T(8,128)} reshape(f32[6144,128]{1,0:T(8,128)} %gather_fusion) | data formatting | bytes 6291456 | tf_op jit(solution)/shard_map/while/body/eval_jaxpr/gather | solution.py:46
  267.4 7.2 %rev.26 = f32[1024,6,128]{2,1,0:T(8,128)} reverse(f32[1024,6,128]{2,1,0:T(8,128)} %reshape.155), dimensions={2} | reverse | bytes 6291456 | tf_op jit(solution)/shard_map/while/body/eval_jaxpr/rev | solution.py:38
  274.7 6.1 %broadcast_select_fusion.6 = f32[1024,6,128]{2,1,0:T(8,128)S(1)} fusion(f32[1024,6,128]{2,1,0:T(8,128)} %rev.26, f32[1024,6,128]{2,1,0:T(8,128)} %reshape.155, pred[1024,6]{1,0:T(8,128)(4,1)S(1)} %get-tuple-element.322), kind=kLoop, calls=%fused_computation.8.clone.1 | loop fusion | flops 786432 | bytes 9443328 | tf_op jit(solution)/shard_map/while/body/eval_jaxpr/jit(_where)/select_n | solution.py:38
  282.1 3.3 maximum_select_fusion.6
  294.9 8.0 %collective-permute-done = f32[1024,128]{1,0:T(8,128)S(1)} collective-permute-done((f32[1024,128]{1,0:T(8,128)}, f32[1024,128]{1,0:T(8,128)S(1)}, u32[]{:S(2)}, u32[]{:S(2)}) %collective-permute-start) | collective-permute-done | bytes 524320 | tf_op jit(solution)/shard_map/while/body/eval_jaxpr/ppermute | solution.py:33
  306.2 3.7 collective-permute-done.2
  310.8 21.1 %gather_fusion = f32[6144,128]{1,0:T(8,128)} fusion(f32[1280,128]{1,0:T(8,128)S(1)} %pad_maximum_fusion.6, s32[6144]{0:T(1024)S(1)} %broadcast_clamp_fusion.3), kind=kCustom, calls=%fused_computation.clone.1 | custom fusion | bytes 6316032 | tf_op jit(solution)/shard_map/while/body/eval_jaxpr/gather | solution.py:46
  331.9 4.6 %reshape.155 = f32[1024,6,128]{2,1,0:T(8,128)} reshape(f32[6144,128]{1,0:T(8,128)} %gather_fusion) | data formatting | bytes 6291456 | tf_op jit(solution)/shard_map/while/body/eval_jaxpr/gather | solution.py:46
  336.4 7.2 %rev.26 = f32[1024,6,128]{2,1,0:T(8,128)} reverse(f32[1024,6,128]{2,1,0:T(8,128)} %reshape.155), dimensions={2} | reverse | bytes 6291456 | tf_op jit(solution)/shard_map/while/body/eval_jaxpr/rev | solution.py:38
  343.7 6.1 %broadcast_select_fusion.6 = f32[1024,6,128]{2,1,0:T(8,128)S(1)} fusion(f32[1024,6,128]{2,1,0:T(8,128)} %rev.26, f32[1024,6,128]{2,1,0:T(8,128)} %reshape.155, pred[1024,6]{1,0:T(8,128)(4,1)S(1)} %get-tuple-element.322), kind=kLoop, calls=%fused_computation.8.clone.1 | loop fusion | flops 786432 | bytes 9443328 | tf_op jit(solution)/shard_map/while/body/eval_jaxpr/jit(_where)/select_n | solution.py:38
  351.1 3.3 maximum_select_fusion.6
  363.4 8.6 %collective-permute-done = f32[1024,128]{1,0:T(8,128)S(1)} collective-permute-done((f32[1024,128]{1,0:T(8,128)}, f32[1024,128]{1,0:T(8,128)S(1)}, u32[]{:S(2)}, u32[]{:S(2)}) %collective-permute-start) | collective-permute-done | bytes 524320 | tf_op jit(solution)/shard_map/while/body/eval_jaxpr/ppermute | solution.py:33
  375.7 3.7 collective-permute-done.2
  380.3 21.1 %gather_fusion = f32[6144,128]{1,0:T(8,128)} fusion(f32[1280,128]{1,0:T(8,128)S(1)} %pad_maximum_fusion.6, s32[6144]{0:T(1024)S(1)} %broadcast_clamp_fusion.3), kind=kCustom, calls=%fused_computation.clone.1 | custom fusion | bytes 6316032 | tf_op jit(solution)/shard_map/while/body/eval_jaxpr/gather | solution.py:46
  401.3 4.6 %reshape.155 = f32[1024,6,128]{2,1,0:T(8,128)} reshape(f32[6144,128]{1,0:T(8,128)} %gather_fusion) | data formatting | bytes 6291456 | tf_op jit(solution)/shard_map/while/body/eval_jaxpr/gather | solution.py:46
  405.9 7.2 %rev.26 = f32[1024,6,128]{2,1,0:T(8,128)} reverse(f32[1024,6,128]{2,1,0:T(8,128)} %reshape.155), dimensions={2} | reverse | bytes 6291456 | tf_op jit(solution)/shard_map/while/body/eval_jaxpr/rev | solution.py:38
  413.1 6.1 %broadcast_select_fusion.6 = f32[1024,6,128]{2,1,0:T(8,128)S(1)} fusion(f32[1024,6,128]{2,1,0:T(8,128)} %rev.26, f32[1024,6,128]{2,1,0:T(8,128)} %reshape.155, pred[1024,6]{1,0:T(8,128)(4,1)S(1)} %get-tuple-element.322), kind=kLoop, calls=%fused_computation.8.clone.1 | loop fusion | flops 786432 | bytes 9443328 | tf_op jit(solution)/shard_map/while/body/eval_jaxpr/jit(_where)/select_n | solution.py:38
  420.6 3.3 maximum_select_fusion.6
  (114 shorter events, 76.4 us)
Async XLA Ops:
  0.9 6.4 %collective-permute-start.3 = (f32[128,128]{1,0:T(8,128)S(1)}, f32[128,128]{1,0:T(8,128)S(1)}, u32[]{:S(2)}, u32[]{:S(2)}) collective-permute-start(f32[128,128]{1,0:T(8,128)S(1)} %get-tuple-element.242), channel_id=1, source_target_pairs={{0,1},{1,2},{2,3},{3,4},{4,5},{5,6},{6,7},{7,0},{8,9},{9,10},{10,1... | collective-permute-start | bytes 196616 | tf_op jit(solution)/shard_map/ppermute | solution.py:21
  0.9 6.3 %collective-permute-start.4 = (f32[128,128]{1,0:T(8,128)S(1)}, f32[128,128]{1,0:T(8,128)S(1)}, u32[]{:S(2)}, u32[]{:S(2)}) collective-permute-start(f32[128,128]{1,0:T(8,128)S(1)} %get-tuple-element.243), channel_id=1, source_target_pairs={{1,0},{2,1},{3,2},{4,3},{5,4},{6,5},{7,6},{0,7},{9,8},{10,9},{11,1... | collective-permute-start | bytes 196616 | tf_op jit(solution)/shard_map/ppermute | solution.py:23
  48.7 3.3 copy-start
  48.7 6.0 %copy-start.7 = (f32[128,128]{1,0:T(8,128)S(1)}, f32[128,128]{1,0:T(8,128)}, u32[]{:S(2)}) copy-start(f32[128,128]{1,0:T(8,128)} %param.8) | copy-start | bytes 196612
  52.0 2.7 copy-start.5
  56.1 5.6 %collective-permute-start.5 = (f32[128,128]{1,0:T(8,128)S(1)}, f32[128,128]{1,0:T(8,128)S(1)}, u32[]{:S(2)}, u32[]{:S(2)}) collective-permute-start(f32[128,128]{1,0:T(8,128)S(1)} %get-tuple-element.240), channel_id=1, source_target_pairs={{0,1},{1,2},{2,3},{3,4},{4,5},{5,6},{6,7},{7,0},{8,9},{9,10},{10,1... | collective-permute-start | bytes 196616 | tf_op jit(solution)/shard_map/ppermute | solution.py:21
  56.1 5.9 %collective-permute-start.6 = (f32[128,128]{1,0:T(8,128)S(1)}, f32[128,128]{1,0:T(8,128)S(1)}, u32[]{:S(2)}, u32[]{:S(2)}) collective-permute-start(f32[128,128]{1,0:T(8,128)S(1)} %get-tuple-element.241), channel_id=1, source_target_pairs={{1,0},{2,1},{3,2},{4,3},{5,4},{6,5},{7,6},{0,7},{9,8},{10,9},{11,1... | collective-permute-start | bytes 196616 | tf_op jit(solution)/shard_map/ppermute | solution.py:23
  109.0 5.6 %collective-permute-start.7 = (f32[128,128]{1,0:T(8,128)S(1)}, f32[128,128]{1,0:T(8,128)S(1)}, u32[]{:S(2)}, u32[]{:S(2)}) collective-permute-start(f32[128,128]{1,0:T(8,128)S(1)} %get-tuple-element.238), channel_id=1, source_target_pairs={{0,1},{1,2},{2,3},{3,4},{4,5},{5,6},{6,7},{7,0},{8,9},{9,10},{10,1... | collective-permute-start | bytes 196616 | tf_op jit(solution)/shard_map/ppermute | solution.py:21
  109.0 5.7 %collective-permute-start.8 = (f32[128,128]{1,0:T(8,128)S(1)}, f32[128,128]{1,0:T(8,128)S(1)}, u32[]{:S(2)}, u32[]{:S(2)}) collective-permute-start(f32[128,128]{1,0:T(8,128)S(1)} %get-tuple-element.239), channel_id=1, source_target_pairs={{1,0},{2,1},{3,2},{4,3},{5,4},{6,5},{7,6},{0,7},{9,8},{10,9},{11,1... | collective-permute-start | bytes 196616 | tf_op jit(solution)/shard_map/ppermute | solution.py:23
  158.4 7.1 %copy-start.10 = (s32[1024,6]{0,1:T(8,128)S(1)}, s32[1024,6]{0,1:T(8,128)}, u32[]{:S(2)}) copy-start(s32[1024,6]{0,1:T(8,128)} %param.11) | copy-start | bytes 73732
  161.6 6.7 %copy-start.3 = (f32[1024,128]{1,0:T(8,128)}, f32[1024,128]{1,0:T(8,128)S(1)}, u32[]{:S(2)}) copy-start(f32[1024,128]{1,0:T(8,128)S(1)} %fusion.37) | copy-start | bytes 1572868
  161.6 6.7 %collective-permute-start.10 = (f32[128,128]{1,0:T(8,128)S(1)}, f32[128,128]{1,0:T(8,128)S(1)}, u32[]{:S(2)}, u32[]{:S(2)}) collective-permute-start(f32[128,128]{1,0:T(8,128)S(1)} %get-tuple-element.237), channel_id=1, source_target_pairs={{1,0},{2,1},{3,2},{4,3},{5,4},{6,5},{7,6},{0,7},{9,8},{10,9},{11,1... | collective-permute-start | bytes 196616 | tf_op jit(solution)/shard_map/ppermute | solution.py:23
  165.3 5.7 %collective-permute-start.9 = (f32[128,128]{1,0:T(8,128)S(1)}, f32[128,128]{1,0:T(8,128)S(1)}, u32[]{:S(2)}, u32[]{:S(2)}) collective-permute-start(f32[128,128]{1,0:T(8,128)S(1)} %get-tuple-element.236), channel_id=1, source_target_pairs={{0,1},{1,2},{2,3},{3,4},{4,5},{5,6},{6,7},{7,0},{8,9},{9,10},{10,1... | collective-permute-start | bytes 196616 | tf_op jit(solution)/shard_map/ppermute | solution.py:21
  215.7 2.7 copy-start.4
  215.7 2.7 copy-start.6
  215.7 2.7 copy-start.9
  219.0 1.0 copy-start.1
  220.2 12.6 %collective-permute-start = (f32[1024,128]{1,0:T(8,128)}, f32[1024,128]{1,0:T(8,128)S(1)}, u32[]{:S(2)}, u32[]{:S(2)}) collective-permute-start(f32[1024,128]{1,0:T(8,128)} %get-tuple-element.338), channel_id=1, source_target_pairs={{0,8},{8,16},{16,24},{1,9},{9,17},{17,25},{2,10},{10,18},{18,26},{... | collective-permute-start | bytes 1572872 | tf_op jit(solution)/shard_map/while/body/eval_jaxpr/ppermute | solution.py:33
  232.8 4.4 %collective-permute-start.1 = (f32[128,128]{1,0:T(8,128)S(1)}, f32[128,128]{1,0:T(8,128)S(1)}, u32[]{:S(2)}, u32[]{:S(2)}) collective-permute-start(f32[128,128]{1,0:T(8,128)S(1)} %get-tuple-element.320), channel_id=1, source_target_pairs={{1,0},{2,1},{3,2},{4,3},{5,4},{6,5},{7,6},{0,7},{9,8},{10,9},{11,1... | collective-permute-start | bytes 196616 | tf_op jit(solution)/shard_map/while/body/eval_jaxpr/ppermute | solution.py:23
  235.3 5.6 %collective-permute-start.2 = (f32[128,128]{1,0:T(8,128)S(1)}, f32[128,128]{1,0:T(8,128)}, u32[]{:S(2)}, u32[]{:S(2)}) collective-permute-start(f32[128,128]{1,0:T(8,128)S(1)} %get-tuple-element.321), channel_id=1, source_target_pairs={{0,1},{1,2},{2,3},{3,4},{4,5},{5,6},{6,7},{7,0},{8,9},{9,10},{10,1... | collective-permute-start | bytes 196616 | tf_op jit(solution)/shard_map/while/body/eval_jaxpr/ppermute | solution.py:21
  285.4 2.7 copy-start.2
  285.4 4.9 %copy-start.8 = (f32[128,128]{1,0:T(8,128)S(1)}, f32[128,128]{1,0:T(8,128)}, u32[]{:S(2)}) copy-start(f32[128,128]{1,0:T(8,128)} %get-tuple-element.371) | copy-start | bytes 196612 | tf_op jit(solution)/shard_map/while
  290.3 12.6 %collective-permute-start = (f32[1024,128]{1,0:T(8,128)}, f32[1024,128]{1,0:T(8,128)S(1)}, u32[]{:S(2)}, u32[]{:S(2)}) collective-permute-start(f32[1024,128]{1,0:T(8,128)} %get-tuple-element.338), channel_id=1, source_target_pairs={{0,8},{8,16},{16,24},{1,9},{9,17},{17,25},{2,10},{10,18},{18,26},{... | collective-permute-start | bytes 1572872 | tf_op jit(solution)/shard_map/while/body/eval_jaxpr/ppermute | solution.py:33
  303.0 3.3 collective-permute-start.1
  304.3 5.6 %collective-permute-start.2 = (f32[128,128]{1,0:T(8,128)S(1)}, f32[128,128]{1,0:T(8,128)}, u32[]{:S(2)}, u32[]{:S(2)}) collective-permute-start(f32[128,128]{1,0:T(8,128)S(1)} %get-tuple-element.321), channel_id=1, source_target_pairs={{0,1},{1,2},{2,3},{3,4},{4,5},{5,6},{6,7},{7,0},{8,9},{9,10},{10,1... | collective-permute-start | bytes 196616 | tf_op jit(solution)/shard_map/while/body/eval_jaxpr/ppermute | solution.py:21
  354.4 2.7 copy-start.2
  354.4 4.9 %copy-start.8 = (f32[128,128]{1,0:T(8,128)S(1)}, f32[128,128]{1,0:T(8,128)}, u32[]{:S(2)}) copy-start(f32[128,128]{1,0:T(8,128)} %get-tuple-element.371) | copy-start | bytes 196612 | tf_op jit(solution)/shard_map/while
  359.3 12.6 %collective-permute-start = (f32[1024,128]{1,0:T(8,128)}, f32[1024,128]{1,0:T(8,128)S(1)}, u32[]{:S(2)}, u32[]{:S(2)}) collective-permute-start(f32[1024,128]{1,0:T(8,128)} %get-tuple-element.338), channel_id=1, source_target_pairs={{0,8},{8,16},{16,24},{1,9},{9,17},{17,25},{2,10},{10,18},{18,26},{... | collective-permute-start | bytes 1572872 | tf_op jit(solution)/shard_map/while/body/eval_jaxpr/ppermute | solution.py:33
  371.9 3.7 collective-permute-start.1
  373.8 5.6 %collective-permute-start.2 = (f32[128,128]{1,0:T(8,128)S(1)}, f32[128,128]{1,0:T(8,128)}, u32[]{:S(2)}, u32[]{:S(2)}) collective-permute-start(f32[128,128]{1,0:T(8,128)S(1)} %get-tuple-element.321), channel_id=1, source_target_pairs={{0,1},{1,2},{2,3},{3,4},{4,5},{5,6},{6,7},{7,0},{8,9},{9,10},{10,1... | collective-permute-start | bytes 196616 | tf_op jit(solution)/shard_map/while/body/eval_jaxpr/ppermute | solution.py:21
  423.9 2.7 copy-start.2
  423.9 4.9 %copy-start.8 = (f32[128,128]{1,0:T(8,128)S(1)}, f32[128,128]{1,0:T(8,128)}, u32[]{:S(2)}) copy-start(f32[128,128]{1,0:T(8,128)} %get-tuple-element.371) | copy-start | bytes 196612 | tf_op jit(solution)/shard_map/while
where the time goes:
time: 438 us; the launch traced here: 429 us
  local copies, waits for them, and re-layouts  246 us (56%)
  other arithmetic  77.5 us (18%)
  waiting for transfers between devices  46.9 us (11%)
  starting transfers between devices  28.9 us (7%)
  matrix products  28.3 us (6%)
    gather x14, local copies, waits for them, and re-layouts, operate(): extended[places]  179 us
    rev x7, local copies, waits for them, and re-layouts, twist_rows(): gathered[..., ::-1]  50.7 us
    select_n x7, other arithmetic, twist_rows(): jnp.where((orient_ids % 2 == 1)[..., None], gathered[..., ::-1], gathered)  42.7 us
    ppermute x3, waiting for transfers between devices, from_behind(): return lax.ppermute(block, axis, route)  23.7 us
    select_n x7, other arithmetic, twist_rows(): jnp.where((orient_ids // 2 == 1)[..., None], jnp.roll(flipped, node_count...  22.9 us
    ppermute x7, starting transfers between devices, padded(): lax.ppermute(head, axis, [((i + 1) % count, i) for i in range(count)])  20.7 us
    dot_general x7, matrix products, operate(): jnp.dot(faces, face_lifts.reshape(6 * node_count, node_count), precision=...  18.5 us
    ppermute x7, waiting for transfers between devices, padded(): lax.ppermute(tail, axis, [(i, (i + 1) % count) for i in range(count)])  17 us
  transfers between devices with their start and end apart: 17, of which 14 were waited for; matrix products, arithmetic and copies ran while one was open for 3% of the time, Pallas kernels for 0%

commit v1 on v0

v1 whole, which is shorter than its diff:
```python
import functools

import jax
import jax.numpy as jnp
import numpy as np
from jax import lax
from jax.experimental import pallas as pl
from jax.experimental.pallas import tpu as pltpu
from jax.sharding import PartitionSpec as P

REACH = 128
STEPS = 4
FACES = 6
BLOCK = 256
WINDOW = BLOCK + 2 * REACH

FINE = [81 / 256, 108 / 256, 54 / 256, 12 / 256, 1 / 256]
DIFF = [81 / 256, -148 / 256, 54 / 256, 12 / 256, 1 / 256]

MESH = pl.DeviceIdType.MESH
F32 = jnp.float32
BF16 = jnp.bfloat16


def twist_basis(nodes):
    quarter = nodes // 4
    basis = np.zeros((nodes, nodes), np.float32)
    for column in range(nodes):
        kind, rep = divmod(column, quarter)
        flip, turn = kind & 1, kind >> 1
        half = nodes // 2
        for a in range(2):
            for b in range(2):
                row = nodes - 1 - rep if a else rep
                row = (row + half) % nodes if b else row
                basis[row, column] = 0.5 * (-1) ** (flip * a + turn * b)
    return basis


def split(x):
    hi = x.astype(BF16)
    return hi, (x - hi.astype(F32)).astype(BF16)


def pair(x):
    return jnp.concatenate(split(x), axis=-1)


def kernel(
    times, ring, starts, volume, lifts, nbr, orient, basis, basis_t, out,
    got, coded, ybf, hot, signs, weights, there, back, out_edge, in_edge,
    s_send, s_recv, e_send, e_recv,
):
    rows, nodes = starts.shape[1], starts.shape[2]
    blocks = rows // BLOCK
    n = lax.axis_index("tm")
    me = lax.axis_index("space")
    right, left = lax.rem(me + 1, ring), lax.rem(me + ring - 1, ring)

    barrier = pltpu.get_barrier_semaphore()
    for side in (left, right):
        pl.semaphore_signal(barrier, inc=1, device_id={"space": side}, device_id_type=MESH)
    for step in range(1, times):
        pl.semaphore_signal(
            barrier, inc=1, device_id={"tm": lax.rem(n + step, times)}, device_id_type=MESH
        )
    pl.semaphore_wait(barrier, times + 1)

    def start_copy(source, target):
        return pltpu.make_async_remote_copy(
            src_ref=starts.at[0],
            dst_ref=got.at[source],
            send_sem=s_send.at[target],
            recv_sem=s_recv.at[source],
            device_id={"tm": target},
            device_id_type=MESH,
        )

    for back_step in range(times - 1):
        target = times - 1 - back_step

        @pl.when(n < target)
        def _():
            start_copy(n, target).start()

    def operator(a):
        full = jnp.dot(
            basis_t[...],
            jnp.dot(a, basis[...], precision=lax.Precision.HIGHEST, preferred_element_type=F32),
            precision=lax.Precision.HIGHEST,
            preferred_element_type=F32,
        )
        wide = pair(full)
        return jnp.concatenate([wide, wide], axis=0)

    for f in range(FACES):
        weights[f] = operator(lifts[f])
    weights[FACES] = operator(volume[...])
    there[...] = jnp.concatenate([basis[...], basis[...]], axis=0).astype(BF16)
    back[...] = jnp.concatenate([basis_t[...], basis_t[...]], axis=0).astype(BF16)

    total = rows * ring
    lane = lax.broadcasted_iota(jnp.int32, (BLOCK, nodes), 1) // (nodes // 4)
    flip, turn = lane % 2, lane // 2
    column = lax.broadcasted_iota(jnp.int32, (BLOCK, WINDOW), 1)
    local = lax.broadcasted_iota(jnp.int32, (BLOCK, FACES), 0)

    def prepare(b, carry):
        at = pl.ds(pl.multiple_of(b * BLOCK, BLOCK), BLOCK)
        offset = nbr[at, :] - (me * rows + b * BLOCK + local)
        offset = jnp.where(offset > REACH, offset - total, offset)
        offset = jnp.where(offset < -REACH, offset + total, offset)
        place = local + REACH + offset
        kind = orient[at, :]
        for f in range(FACES):
            hot[b, f] = jnp.where(column == place[:, f : f + 1], 1.0, 0.0).astype(BF16)
            o = kind[:, f : f + 1]
            odd = (flip * (o % 2) + turn * (o // 2)) % 2
            signs[b, f] = (1 - 2 * odd).astype(F32).astype(BF16)
        return carry

    lax.fori_loop(0, blocks, prepare, 0)

    def encode(j, source):
        def body(b, carry):
            at = pl.ds(pl.multiple_of(b * BLOCK, BLOCK), BLOCK)
            coded[j, at, :] = jnp.dot(pair(source(at)), there[...], preferred_element_type=F32)
            return carry

        lax.fori_loop(0, blocks, body, 0)

    encode(n, lambda at: starts[0, at, :])

    def arrive(j):
        @pl.when(j < n)
        def _():
            start_copy(j, n).wait_recv()
            encode(j, lambda at: got[j, at, :])

    def forcing(step, at):
        acc = None
        for i in range(STEPS + 1):
            j = step - STEPS + i
            coef = jnp.where(j == 0, FINE[i], DIFF[i]).astype(F32)
            coef = jnp.where(jnp.logical_and(j >= 0, j <= n), coef, 0.0)
            term = coef * coded[jnp.clip(j, 0, n), at, :]
            acc = term if acc is None else acc + term
        return acc

    def edge_copy(step, side):
        return pltpu.make_async_remote_copy(
            src_ref=out_edge.at[step, side],
            dst_ref=in_edge.at[step, 1 - side],
            send_sem=e_send.at[step, side],
            recv_sem=e_recv.at[step, 1 - side],
            device_id={"space": right if side else left},
            device_id_type=MESH,
        )

    last = n + STEPS

    def finish(step, slot, b, y):
        ybf[slot, pl.ds(REACH + b * BLOCK, BLOCK), :] = pair(y)

        @pl.when(step < last)
        def _():
            if b == 0:
                out_edge[step, 0] = y[:REACH]
                edge_copy(step, 0).start()
            if b == blocks - 1:
                out_edge[step, 1] = y[BLOCK - REACH :]
                edge_copy(step, 1).start()

    order = list(range(1, blocks - 1)) + [0, blocks - 1]

    arrive(0)
    for b in order:
        finish(0, 0, b, forcing(0, pl.ds(b * BLOCK, BLOCK)))

    def advance(step, carry):
        now = lax.rem(step, 2)
        before = 1 - now
        arrive(step)
        for place, b in enumerate(order):
            if place == blocks - 2:
                for side in range(2):
                    edge_copy(step - 1, 1 - side).wait_recv()
                    at = REACH + rows if side else 0
                    ybf[before, pl.ds(at, REACH), :] = pair(in_edge[step - 1, side])
            window = ybf[before, pl.ds(b * BLOCK, WINDOW), :]
            acc = jnp.dot(
                ybf[before, pl.ds(REACH + b * BLOCK, BLOCK), :],
                weights[FACES],
                preferred_element_type=F32,
            )
            for f in range(FACES):
                seen = jnp.dot(hot[b, f], window, preferred_element_type=F32).astype(BF16)
                sign = signs[b, f]
                seen = seen * jnp.concatenate([sign, sign], axis=-1)
                acc = acc + jnp.dot(seen, weights[f], preferred_element_type=F32)
            y = acc[:, :nodes] + acc[:, nodes:] + forcing(step, pl.ds(b * BLOCK, BLOCK))
            finish(step, now, b, y)
        for side in range(2):
            edge_copy(step - 1, side).wait_send()
        return carry

    lax.fori_loop(1, last + 1, advance, 0)

    final = lax.rem(last, 2)

    def decode(b, carry):
        at = pl.ds(pl.multiple_of(REACH + b * BLOCK, REACH), BLOCK)
        to = pl.ds(pl.multiple_of(b * BLOCK, BLOCK), BLOCK)
        out[0, to, :] = jnp.dot(ybf[final, at, :], back[...], preferred_element_type=F32)
        return carry

    lax.fori_loop(0, blocks, decode, 0)

    for target in range(1, times):

        @pl.when(n < target)
        def _():
            start_copy(n, target).wait_send()


def solution(mesh):
    times, ring = mesh.shape["tm"], mesh.shape["space"]

    def per_device(starts, volume_op, face_lifts, neighbours, orientation):
        rows, nodes = starts.shape[1], starts.shape[2]
        blocks = rows // BLOCK
        steps = times + STEPS
        basis = jnp.asarray(twist_basis(nodes))
        basis_t = jnp.asarray(twist_basis(nodes).T.copy())
        return pl.pallas_call(
            functools.partial(kernel, times, ring),
            out_shape=jax.ShapeDtypeStruct(starts.shape, F32),
            in_specs=[pl.BlockSpec(memory_space=pltpu.VMEM)] * 7,
            out_specs=pl.BlockSpec(memory_space=pltpu.VMEM),
            scratch_shapes=[
                pltpu.VMEM((times, rows, nodes), F32),
                pltpu.VMEM((times, rows, nodes), F32),
                pltpu.VMEM((2, rows + 2 * REACH, 2 * nodes), BF16),
                pltpu.VMEM((blocks, FACES, BLOCK, WINDOW), BF16),
                pltpu.VMEM((blocks, FACES, BLOCK, nodes), BF16),
                pltpu.VMEM((FACES + 1, 2 * nodes, 2 * nodes), BF16),
                pltpu.VMEM((2 * nodes, nodes), BF16),
                pltpu.VMEM((2 * nodes, nodes), BF16),
                pltpu.VMEM((steps, 2, REACH, nodes), F32),
                pltpu.VMEM((steps, 2, REACH, nodes), F32),
                pltpu.SemaphoreType.DMA((times,)),
                pltpu.SemaphoreType.DMA((times,)),
                pltpu.SemaphoreType.DMA((steps, 2)),
                pltpu.SemaphoreType.DMA((steps, 2)),
            ],
            compiler_params=pltpu.CompilerParams(
                collective_id=0, has_side_effects=True, vmem_limit_bytes=50 * 1024 * 1024
            ),
        )(starts, volume_op, face_lifts, neighbours, orientation, basis, basis_t)

    return jax.shard_map(
        per_device,
        mesh=mesh,
        in_specs=(P("tm", "space", None), P(), P(), P("space", None), P("space", None)),
        out_specs=P("tm", "space", None),
        check_vma=False,
    )
```

time: 438 us -> 67.3 us (0.15)
  the two profiles are of different devices: /device:TPU:4 before, /device:TPU:6 now
where the time goes in v1:
time: 67.3 us; the launch traced here: 67.1 us
  Pallas kernels  64.2 us (95%)
  local copies, waits for them, and re-layouts  2.88 us (4%)
    pallas_call x1, Pallas kernels, per_device(): pl.pallas_call(functools.partial(kernel, times, ring), out_shape=jax.Shap...  64.2 us
    unnamed x13, local copies, waits for them, and re-layouts  2.88 us

profile of v1, /device:TPU:6, one launch (start us, length us, event | category | flops | bytes accessed | tf_op | source)
XLA Modules:
  0.0 67.1 jit_solution(8922823921821236211)
XLA Ops:
  0.0 0.0 copy-start
  0.0 0.0 copy-start.4
  0.0 1.0 %copy.8.nbr = s32[1024,6]{1,0:T(8,128)S(1)} copy(s32[1024,6]{0,1:T(8,128)} %param.10) | data formatting | bytes 49152 | tf_op args[3]
  1.0 0.0 copy-start.1
  1.1 0.0 copy-start.2
  1.1 0.0 copy-start.3
  1.1 1.0 %copy.9.orient = s32[1024,6]{1,0:T(8,128)S(1)} copy(s32[1024,6]{0,1:T(8,128)} %param.11) | data formatting | bytes 49152 | tf_op args[4]
  2.1 0.0 copy-done
  2.1 0.0 copy-done.4
  2.1 0.0 copy-done.1
  2.1 0.0 copy-done.2
  2.2 0.0 copy-done.3
  2.2 64.2 %shard_map.73 = f32[1,1024,128]{2,1,0:T(8,128)S(1)} custom-call(f32[1,1024,128]{2,1,0:T(8,128)S(1)} %copy-done, f32[128,128]{1,0:T(8,128)S(1)} %copy-done.2, f32[6,128,128]{2,1,0:T(8,128)S(1)} %copy-done.1, s32[1024,6]{1,0:T(8,128)S(1)} %copy.8.nbr, s32[1024,6]{1,0:T(8,128)S(1)} %copy.9.orient, f32[128,128]{1,0:T(8,128)S(1)} %copy-done.4, ...), custom_call_target="tpu_custom_call" | custom-call | tf_op jit(solution)/shard_map/pallas_call | solution.py:235
  66.3 0.8 %copy.11 = f32[1,1024,128]{2,1,0:T(8,128)} copy(f32[1,1024,128]{2,1,0:T(8,128)S(1)} %shard_map.73) | data formatting | bytes 1048576
Async XLA Ops:
  0.0 2.1 %copy-start = (f32[1,1024,128]{2,1,0:T(8,128)S(1)}, f32[1,1024,128]{2,1,0:T(8,128)}, u32[]{:S(2)}) copy-start(f32[1,1024,128]{2,1,0:T(8,128)} %starts.1) | copy-start | bytes 1572868
  0.0 2.1 %copy-start.4 = (f32[128,128]{1,0:T(8,128)S(1)}, f32[128,128]{1,0:T(8,128)}, u32[]{:S(2)}) copy-start(f32[128,128]{1,0:T(8,128)} %constant.4.clone.basis) | copy-start | bytes 196612
  1.0 1.1 %copy-start.1 = (f32[6,128,128]{2,1,0:T(8,128)S(1)}, f32[6,128,128]{2,1,0:T(8,128)}, u32[]{:S(2)}) copy-start(f32[6,128,128]{2,1,0:T(8,128)} %lifts.1) | copy-start | bytes 1179652
  1.1 1.1 %copy-start.2 = (f32[128,128]{1,0:T(8,128)S(1)}, f32[128,128]{1,0:T(8,128)}, u32[]{:S(2)}) copy-start(f32[128,128]{1,0:T(8,128)} %volume.1) | copy-start | bytes 196612
  1.1 1.1 %copy-start.3 = (f32[128,128]{1,0:T(8,128)S(1)}, f32[128,128]{1,0:T(8,128)}, u32[]{:S(2)}) copy-start(f32[128,128]{1,0:T(8,128)} %constant.5.clone.basis_t) | copy-start | bytes 196612

commit v2 on v1

v2 whole, which is shorter than its diff:
```python
import functools

import jax
import jax.numpy as jnp
import numpy as np
from jax import lax
from jax.experimental import pallas as pl
from jax.experimental.pallas import tpu as pltpu
from jax.sharding import PartitionSpec as P

REACH = 128
STEPS = 4
FACES = 6
BLOCK = 256
WINDOW = BLOCK + 2 * REACH

FINE = [81 / 256, 108 / 256, 54 / 256, 12 / 256, 1 / 256]
DIFF = [81 / 256, -148 / 256, 54 / 256, 12 / 256, 1 / 256]

MESH = pl.DeviceIdType.MESH
F32 = jnp.float32
BF16 = jnp.bfloat16


def twist_basis(nodes):
    quarter = nodes // 4
    basis = np.zeros((nodes, nodes), np.float32)
    for column in range(nodes):
        kind, rep = divmod(column, quarter)
        flip, turn = kind & 1, kind >> 1
        half = nodes // 2
        for a in range(2):
            for b in range(2):
                row = nodes - 1 - rep if a else rep
                row = (row + half) % nodes if b else row
                basis[row, column] = 0.5 * (-1) ** (flip * a + turn * b)
    return basis


def split(x):
    hi = x.astype(BF16)
    return hi, (x - hi.astype(F32)).astype(BF16)


def pair(x):
    return jnp.concatenate(split(x), axis=-1)


def kernel(
    times, ring, starts, volume, lifts, nbr, orient, basis_t, out,
    got, coded, state, halves, hot, place, signs, wide, low, out_edge, in_edge,
    s_send, s_recv, e_send, e_recv,
):
    rows, nodes = starts.shape[1], starts.shape[2]
    blocks, tiles = rows // BLOCK, rows // REACH
    n = lax.axis_index("tm")
    me = lax.axis_index("space")
    right, left = lax.rem(me + 1, ring), lax.rem(me + ring - 1, ring)

    barrier = pltpu.get_barrier_semaphore()
    for side in (left, right):
        pl.semaphore_signal(barrier, inc=1, device_id={"space": side}, device_id_type=MESH)
    for step in range(1, times):
        pl.semaphore_signal(
            barrier, inc=1, device_id={"tm": lax.rem(n + step, times)}, device_id_type=MESH
        )
    pl.semaphore_wait(barrier, times + 1)

    order = list(range(1, blocks - 1)) + [0, blocks - 1]
    square = times == 4 and blocks == 4

    def rows_of(b):
        return pl.ds(pl.multiple_of(b * BLOCK, BLOCK), BLOCK)

    def send(source, b, target, own):
        held = starts.at[0] if own else got.at[source]
        return pltpu.make_async_remote_copy(
            src_ref=held.at[rows_of(b)],
            dst_ref=got.at[source, rows_of(b)],
            send_sem=s_send.at[target, source, b],
            recv_sem=s_recv.at[source, b],
            device_id={"tm": target},
            device_id_type=MESH,
        )

    own_hops, passed_hops = [], []
    if square:
        for b in range(blocks):
            own_hops += [(0, 0, b, 1), (0, 0, b, 2), (1, 1, b, 3), (2, 2, b, 3)]
            passed_hops += [(1 if b < 2 else 2, 0, b, 3), (3, 1, b, 2)]
        first = [(0, 1, 0), (2, 2, 0), (1, 1, 0), (3, 2, 0), (2, 1, 0), (0, 2, 0), (3, 1, 0), (1, 2, 0)]

        @pl.when(n == 0)
        def _():
            for b, target, source in first:
                send(source, b, target, True).start()

        for early in (1, 2):

            @pl.when(n == early)
            def _():
                send(early, order[0], 3, True).start()
    else:
        for target in range(times - 1, 0, -1):

            @pl.when(n < target)
            def _():
                for b in order:
                    send(n, b, target, True).start()

    turn_in = basis_t[...].astype(BF16)
    turn_in = jnp.concatenate([turn_in, turn_in], axis=1)

    def rotate(x):
        return lax.dot_general(turn_in, pair(x), (((1,), (1,)), ((), ())), preferred_element_type=F32)

    def operator(a):
        return split(rotate(jnp.dot(turn_in, jnp.concatenate(split(a), axis=0), preferred_element_type=F32)))

    for p in range(FACES // 2):
        h0, l0 = operator(lifts[2 * p])
        h1, l1 = operator(lifts[2 * p + 1])
        high = jnp.concatenate([h0, h1], axis=1)
        wide[p] = jnp.concatenate([high, jnp.concatenate([l0, l1], axis=1)], axis=0)
        low[p] = high
    hv, lv = operator(volume[...])
    wide[FACES // 2] = jnp.concatenate(
        [jnp.concatenate([hv, hv], axis=1), jnp.concatenate([lv, lv], axis=1)], axis=0
    )

    total = rows * ring
    lane = lax.broadcasted_iota(jnp.int32, (FACES, REACH), 1)
    for t in range(tiles):
        at = pl.ds(t * REACH, REACH)
        offset = nbr[:, at] - (me * rows + t * REACH + lane)
        offset = jnp.where(offset > REACH, offset - total, offset)
        offset = jnp.where(offset < -REACH, offset + total, offset)
        place[t] = lane + REACH + offset
        o = orient[:, at]
        signs[t, 0] = (1 - 2 * (o % 2)).astype(F32)
        signs[t, 1] = (1 - 2 * (o // 2)).astype(F32)

    column = lax.broadcasted_iota(jnp.int32, (WINDOW, BLOCK), 0)
    for b in range(blocks):
        for p in range(FACES // 2):
            f = pl.ds(2 * p + 1, 1)
            row = jnp.concatenate([place[2 * b, f, :], place[2 * b + 1, f, :] + REACH], axis=1)
            hot[b, p] = jnp.where(column == row, 1.0, 0.0).astype(BF16)

    for b in range(blocks):
        coded[n, b] = rotate(starts[0, rows_of(b), :])

    def arrive(j, b):
        send(j, b, n, False).wait_recv()
        coded[j, b] = rotate(got[j, rows_of(b), :])

    @pl.when(n > 0)
    def _():
        def body(i, carry):
            b = lax.rem(i + jnp.where(n == 2, blocks // 2, 0), blocks)
            send(0, b, n, False).wait_recv()
            if square:

                @pl.when(jnp.logical_and(n < 3, i < 2))
                def _():
                    send(0, b, 3, False).start()

            coded[0, b] = rotate(got[0, rows_of(b), :])
            return carry

        lax.fori_loop(0, blocks, body, 0)

    if square:
        for later in (1, 2):

            @pl.when(n == later)
            def _():
                for b in order[1:]:
                    send(later, b, 3, True).start()

    def forcing(step, b):
        acc = None
        for i in range(STEPS + 1):
            j = step - STEPS + i
            coef = jnp.where(j == 0, FINE[i], DIFF[i]).astype(F32)
            coef = jnp.where(jnp.logical_and(j >= 0, j <= n), coef, 0.0)
            term = coef * coded[jnp.clip(j, 0, n), b]
            acc = term if acc is None else acc + term
        return acc

    def edge_copy(step, side):
        return pltpu.make_async_remote_copy(
            src_ref=out_edge.at[step, side],
            dst_ref=in_edge.at[step, 1 - side],
            send_sem=e_send.at[step, side],
            recv_sem=e_recv.at[step, 1 - side],
            device_id={"space": right if side else left},
            device_id_type=MESH,
        )

    last = n + STEPS

    def finish(step, slot, b, y):
        both = jnp.concatenate(split(y), axis=0)
        for u in range(2):
            state[slot, 2 * b + 1 + u] = y[:, u * REACH : (u + 1) * REACH]
            halves[slot, 2 * b + 1 + u] = both[:, u * REACH : (u + 1) * REACH]

        @pl.when(step < last)
        def _():
            if b == 0:
                out_edge[step, 0] = y[:, :REACH]
                edge_copy(step, 0).start()
            if b == blocks - 1:
                out_edge[step, 1] = y[:, REACH:]
                edge_copy(step, 1).start()

    quarter = nodes // 4

    def seen(slot, t, f):
        at = place[t, pl.ds(f, 1), :]
        inner = at % REACH
        index = jnp.broadcast_to(inner, (nodes, REACH))
        tile = jnp.broadcast_to(at // REACH, (nodes, REACH))
        flip = signs[t, 0, pl.ds(f, 1), :]
        turn = signs[t, 1, pl.ds(f, 1), :]

        def take(k):
            return jnp.take_along_axis(
                state[slot, t + k], index, axis=1, mode="promise_in_bounds"
            )

        v = jnp.where(tile == 0, take(0), jnp.where(tile == 1, take(1), take(2)))
        return twisted(v, flip, turn)

    def twisted(v, flip, turn):
        return jnp.concatenate(
            [
                v[:quarter],
                v[quarter : 2 * quarter] * flip,
                v[2 * quarter : 3 * quarter] * turn,
                v[3 * quarter :] * (flip * turn),
            ],
            axis=0,
        )

    def seen_block(slot, b, p):
        window = jnp.concatenate([halves[slot, 2 * b + i] for i in range(4)], axis=1)
        v = jnp.dot(window, hot[b, p], preferred_element_type=F32)
        f = pl.ds(2 * p + 1, 1)
        flip, turn = [
            jnp.concatenate([signs[2 * b, i, f, :], signs[2 * b + 1, i, f, :]], axis=1)
            for i in range(2)
        ]
        return tuple(
            twisted(part, flip, turn).astype(BF16) for part in (v[:nodes], v[nodes:])
        )

    for b in order:
        finish(0, 0, b, forcing(0, b))

    def advance(step, carry):
        now = lax.rem(step, 2)
        before = 1 - now
        for position, b in enumerate(order):
            if position == blocks - 2:
                for side in range(2):
                    edge_copy(step - 1, 1 - side).wait_recv()
                    edge = in_edge[step - 1, side]
                    state[before, (tiles + 1) * side] = edge
                    halves[before, (tiles + 1) * side] = jnp.concatenate(split(edge), axis=0)
            own = jnp.concatenate([halves[before, 2 * b + 1], halves[before, 2 * b + 2]], axis=1)
            acc = jnp.dot(wide[FACES // 2], own, preferred_element_type=F32)
            rest = None
            for p in range(FACES // 2):
                parts = [
                    split(
                        jnp.concatenate(
                            [seen(before, 2 * b, 2 * p), seen(before, 2 * b + 1, 2 * p)], axis=1
                        )
                    ),
                    seen_block(before, b, p),
                ]
                high = jnp.concatenate([parts[0][0], parts[1][0]], axis=0)
                tail = jnp.concatenate([parts[0][1], parts[1][1]], axis=0)
                acc = acc + jnp.dot(wide[p], high, preferred_element_type=F32)
                more = jnp.dot(low[p], tail, preferred_element_type=F32)
                rest = more if rest is None else rest + more

            @pl.when(step < n)
            def _():
                arrive(step, b)
                if square:

                    @pl.when(jnp.logical_and(n == 3, step == 1))
                    def _():
                        send(1, b, 2, False).start()

            finish(step, now, b, acc[:nodes] + acc[nodes:] + rest + forcing(step, b))
        for side in range(2):
            edge_copy(step - 1, side).wait_send()
        return carry

    lax.fori_loop(1, last + 1, advance, 0)

    final = lax.rem(last, 2)
    turn_out = basis_t[...].astype(BF16)
    turn_out = jnp.concatenate([turn_out, turn_out], axis=0)

    for t in range(tiles):
        out[0, pl.ds(t * REACH, REACH), :] = jnp.dot(
            pair(jnp.transpose(state[final, t + 1])), turn_out, preferred_element_type=F32
        )

    if square:
        for who in range(times):

            @pl.when(n == who)
            def _():
                for hops, own in ((own_hops, True), (passed_hops, False)):
                    for sender, source, b, target in hops:
                        if sender == who:
                            send(source, b, target, own).wait_send()
    else:
        for target in range(1, times):

            @pl.when(n < target)
            def _():
                for b in order:
                    send(n, b, target, True).wait_send()


def solution(mesh):
    times, ring = mesh.shape["tm"], mesh.shape["space"]

    def per_device(starts, volume_op, face_lifts, neighbours, orientation):
        rows, nodes = starts.shape[1], starts.shape[2]
        blocks, tiles = rows // BLOCK, rows // REACH
        steps = times + STEPS
        basis_t = jnp.asarray(twist_basis(nodes).T.copy())
        return pl.pallas_call(
            functools.partial(kernel, times, ring),
            out_shape=jax.ShapeDtypeStruct(starts.shape, F32),
            in_specs=[pl.BlockSpec(memory_space=pltpu.VMEM)] * 6,
            out_specs=pl.BlockSpec(memory_space=pltpu.VMEM),
            scratch_shapes=[
                pltpu.VMEM((times, rows, nodes), F32),
                pltpu.VMEM((times, blocks, nodes, BLOCK), F32),
                pltpu.VMEM((2, tiles + 2, nodes, REACH), F32),
                pltpu.VMEM((2, tiles + 2, 2 * nodes, REACH), BF16),
                pltpu.VMEM((blocks, FACES // 2, WINDOW, BLOCK), BF16),
                pltpu.VMEM((tiles, FACES, REACH), jnp.int32),
                pltpu.VMEM((tiles, 2, FACES, REACH), F32),
                pltpu.VMEM((FACES // 2 + 1, 2 * nodes, 2 * nodes), BF16),
                pltpu.VMEM((FACES // 2, nodes, 2 * nodes), BF16),
                pltpu.VMEM((steps, 2, nodes, REACH), F32),
                pltpu.VMEM((steps, 2, nodes, REACH), F32),
                pltpu.SemaphoreType.DMA((times, times, blocks)),
                pltpu.SemaphoreType.DMA((times, blocks)),
                pltpu.SemaphoreType.DMA((steps, 2)),
                pltpu.SemaphoreType.DMA((steps, 2)),
            ],
            compiler_params=pltpu.CompilerParams(
                collective_id=0, has_side_effects=True, vmem_limit_bytes=50 * 1024 * 1024
            ),
        )(starts, volume_op, face_lifts, neighbours.T, orientation.T, basis_t)

    return jax.shard_map(
        per_device,
        mesh=mesh,
        in_specs=(P("tm", "space", None), P(), P(), P("space", None), P("space", None)),
        out_specs=P("tm", "space", None),
        check_vma=False,
    )
```

time: 67.3 us -> 63.2 us (0.939)
  the two profiles are of different devices: /device:TPU:6 before, /device:TPU:4 now
where the time goes in v2:
time: 63.2 us; the launch traced here: 62.8 us
  Pallas kernels  56.8 us (90%)
  local copies, waits for them, and re-layouts  6.02 us (10%)
    pallas_call x1, Pallas kernels, per_device(): pl.pallas_call(functools.partial(kernel, times, ring), out_shape=jax.Shap...  56.8 us
    unnamed x13, local copies, waits for them, and re-layouts  6.02 us

profile of v2, /device:TPU:4, one launch (start us, length us, event | category | flops | bytes accessed | tf_op | source)
XLA Modules:
  0.0 62.8 jit_solution(6494227094720652418)
XLA Ops:
  0.0 0.0 copy-start
  0.0 1.0 %copy-done = f32[1,1024,128]{2,1,0:T(8,128)S(1)} copy-done((f32[1,1024,128]{2,1,0:T(8,128)S(1)}, f32[1,1024,128]{2,1,0:T(8,128)}, u32[]{:S(2)}) %copy-start) | copy-done | bytes 524312
  1.0 0.0 copy-start.1
  1.0 1.0 %copy-done.1 = f32[6,128,128]{2,1,0:T(8,128)S(1)} copy-done((f32[6,128,128]{2,1,0:T(8,128)S(1)}, f32[6,128,128]{2,1,0:T(8,128)}, u32[]{:S(2)}) %copy-start.1) | copy-done | bytes 393240
  2.0 0.0 copy-start.2
  2.0 0.8 %copy-done.2 = f32[128,128]{1,0:T(8,128)S(1)} copy-done((f32[128,128]{1,0:T(8,128)S(1)}, f32[128,128]{1,0:T(8,128)}, u32[]{:S(2)}) %copy-start.2) | copy-done | bytes 65560
  2.9 0.0 copy-start.3
  2.9 0.8 %copy-done.3 = f32[128,128]{1,0:T(8,128)S(1)} copy-done((f32[128,128]{1,0:T(8,128)S(1)}, f32[128,128]{1,0:T(8,128)}, u32[]{:S(2)}) %copy-start.3) | copy-done | bytes 65560
  3.7 0.0 copy-start.4
  3.7 0.8 %copy-done.4 = s32[1024,6]{0,1:T(8,128)S(1)} copy-done((s32[1024,6]{0,1:T(8,128)S(1)}, s32[1024,6]{0,1:T(8,128)}, u32[]{:S(2)}) %copy-start.4) | copy-done | bytes 24600
  4.5 0.0 copy-start.5
  4.5 0.8 %copy-done.5 = s32[1024,6]{0,1:T(8,128)S(1)} copy-done((s32[1024,6]{0,1:T(8,128)S(1)}, s32[1024,6]{0,1:T(8,128)}, u32[]{:S(2)}) %copy-start.5) | copy-done | bytes 24600
  5.2 56.8 %shard_map.64 = f32[1,1024,128]{2,1,0:T(8,128)S(1)} custom-call(f32[1,1024,128]{2,1,0:T(8,128)S(1)} %copy-done, f32[128,128]{1,0:T(8,128)S(1)} %copy-done.2, f32[6,128,128]{2,1,0:T(8,128)S(1)} %copy-done.1, s32[6,1024]{1,0:T(8,128)S(1)} %bitcast.2, s32[6,1024]{1,0:T(8,128)S(1)} %bitcast.3, f32[128,128]{1,0:T(8,128)S(1)} %copy-done.3), custom_call_target="tpu_custom_call" | custom-call | tf_op jit(solution)/shard_map/pallas_call | solution.py:341
  62.0 0.8 %copy.8 = f32[1,1024,128]{2,1,0:T(8,128)} copy(f32[1,1024,128]{2,1,0:T(8,128)S(1)} %shard_map.64) | data formatting | bytes 1048576
Async XLA Ops:
  0.0 1.0 %copy-start = (f32[1,1024,128]{2,1,0:T(8,128)S(1)}, f32[1,1024,128]{2,1,0:T(8,128)}, u32[]{:S(2)}) copy-start(f32[1,1024,128]{2,1,0:T(8,128)} %starts.1) | copy-start | bytes 1572868
  1.0 1.0 %copy-start.1 = (f32[6,128,128]{2,1,0:T(8,128)S(1)}, f32[6,128,128]{2,1,0:T(8,128)}, u32[]{:S(2)}) copy-start(f32[6,128,128]{2,1,0:T(8,128)} %lifts.1) | copy-start | bytes 1179652
  2.0 0.8 %copy-start.2 = (f32[128,128]{1,0:T(8,128)S(1)}, f32[128,128]{1,0:T(8,128)}, u32[]{:S(2)}) copy-start(f32[128,128]{1,0:T(8,128)} %volume.1) | copy-start | bytes 196612
  2.9 0.8 %copy-start.3 = (f32[128,128]{1,0:T(8,128)S(1)}, f32[128,128]{1,0:T(8,128)}, u32[]{:S(2)}) copy-start(f32[128,128]{1,0:T(8,128)} %constant.2.clone.basis_t) | copy-start | bytes 196612
  3.7 0.8 %copy-start.4 = (s32[1024,6]{0,1:T(8,128)S(1)}, s32[1024,6]{0,1:T(8,128)}, u32[]{:S(2)}) copy-start(s32[1024,6]{0,1:T(8,128)} %param.9) | copy-start | bytes 73732
  4.5 0.8 %copy-start.5 = (s32[1024,6]{0,1:T(8,128)S(1)}, s32[1024,6]{0,1:T(8,128)}, u32[]{:S(2)}) copy-start(s32[1024,6]{0,1:T(8,128)} %param.10) | copy-start | bytes 73732

commit v3 on v2

--- a/solution.py
+++ b/solution.py
@@ -183,8 +183,11 @@
         for i in range(STEPS + 1):
             j = step - STEPS + i
             coef = jnp.where(j == 0, FINE[i], DIFF[i]).astype(F32)
-            coef = jnp.where(jnp.logical_and(j >= 0, j <= n), coef, 0.0)
-            term = coef * coded[jnp.clip(j, 0, n), b]
+            held = jnp.logical_and(j >= 0, j <= n)
+            if i == STEPS:
+                held = jnp.logical_and(held, jnp.logical_or(step >= n, step == 0))
+            place_of = jnp.where(held, j, n)
+            term = jnp.where(held, coef, 0.0) * coded[place_of, b]
             acc = term if acc is None else acc + term
         return acc
 
@@ -200,20 +203,18 @@
 
     last = n + STEPS
 
-    def finish(step, slot, b, y):
+    def store(slot, b, y):
         both = jnp.concatenate(split(y), axis=0)
         for u in range(2):
             state[slot, 2 * b + 1 + u] = y[:, u * REACH : (u + 1) * REACH]
             halves[slot, 2 * b + 1 + u] = both[:, u * REACH : (u + 1) * REACH]
 
+    def send_edges(step, slot):
         @pl.when(step < last)
         def _():
-            if b == 0:
-                out_edge[step, 0] = y[:, :REACH]
-                edge_copy(step, 0).start()
-            if b == blocks - 1:
-                out_edge[step, 1] = y[:, REACH:]
-                edge_copy(step, 1).start()
+            for side in range(2):
+                out_edge[step, side] = state[slot, tiles if side else 1]
+                edge_copy(step, side).start()
 
     quarter = nodes // 4
 
@@ -256,47 +257,58 @@
             twisted(part, flip, turn).astype(BF16) for part in (v[:nodes], v[nodes:])
         )
 
+    def apply(slot, b):
+        own = jnp.concatenate([halves[slot, 2 * b + 1], halves[slot, 2 * b + 2]], axis=1)
+        acc = jnp.dot(wide[FACES // 2], own, preferred_element_type=F32)
+        rest = None
+        for p in range(FACES // 2):
+            parts = [
+                split(
+                    jnp.concatenate(
+                        [seen(slot, 2 * b, 2 * p), seen(slot, 2 * b + 1, 2 * p)], axis=1
+                    )
+                ),
+                seen_block(slot, b, p),
+            ]
+            high = jnp.concatenate([parts[0][0], parts[1][0]], axis=0)
+            tail = jnp.concatenate([parts[0][1], parts[1][1]], axis=0)
+            acc = acc + jnp.dot(wide[p], high, preferred_element_type=F32)
+            more = jnp.dot(low[p], tail, preferred_element_type=F32)
+            rest = more if rest is None else rest + more
+        return acc[:nodes] + acc[nodes:] + rest
+
     for b in order:
-        finish(0, 0, b, forcing(0, b))
+        store(0, b, forcing(0, b))
+    send_edges(0, 0)
 
     def advance(step, carry):
         now = lax.rem(step, 2)
         before = 1 - now
-        for position, b in enumerate(order):
-            if position == blocks - 2:
+        for region in (order[:-2], order[-2:]):
+            if region[0] == 0:
                 for side in range(2):
                     edge_copy(step - 1, 1 - side).wait_recv()
                     edge = in_edge[step - 1, side]
                     state[before, (tiles + 1) * side] = edge
                     halves[before, (tiles + 1) * side] = jnp.concatenate(split(edge), axis=0)
-            own = jnp.concatenate([halves[before, 2 * b + 1], halves[before, 2 * b + 2]], axis=1)
-            acc = jnp.dot(wide[FACES // 2], own, preferred_element_type=F32)
-            rest = None
-            for p in range(FACES // 2):
-                parts = [
-                    split(
-                        jnp.concatenate(
-                            [seen(before, 2 * b, 2 * p), seen(before, 2 * b + 1, 2 * p)], axis=1
-                        )
-                    ),
-                    seen_block(before, b, p),
-                ]
-                high = jnp.concatenate([parts[0][0], parts[1][0]], axis=0)
-                tail = jnp.concatenate([parts[0][1], parts[1][1]], axis=0)
-                acc = acc + jnp.dot(wide[p], high, preferred_element_type=F32)
-                more = jnp.dot(low[p], tail, preferred_element_type=F32)
-                rest = more if rest is None else rest + more
+            made = [apply(before, b) + forcing(step, b) for b in region]
+            for b, y in zip(region, made):
+                store(now, b, y)
 
             @pl.when(step < n)
             def _():
-                arrive(step, b)
-                if square:
-
-                    @pl.when(jnp.logical_and(n == 3, step == 1))
-                    def _():
-                        send(1, b, 2, False).start()
-
-            finish(step, now, b, acc[:nodes] + acc[nodes:] + rest + forcing(step, b))
+                for b in region:
+                    arrive(step, b)
+                    if square:
+
+                        @pl.when(jnp.logical_and(n == 3, step == 1))
+                        def _():
+                            send(1, b, 2, False).start()
+
+                    y = jnp.concatenate([state[now, 2 * b + 1], state[now, 2 * b + 2]], axis=1)
+                    store(now, b, y + DIFF[STEPS] * coded[step, b])
+
+        send_edges(step, now)
         for side in range(2):
             edge_copy(step - 1, side).wait_send()
         return carry

time: 63.2 us -> 63 us (level)
  no operation moved by 1% of the time
where the time goes in v3:
time: 63 us; the launch traced here: 62.2 us
  Pallas kernels  56.2 us (89%)
  local copies, waits for them, and re-layouts  6.02 us (10%)
    pallas_call x1, Pallas kernels, per_device(): pl.pallas_call(functools.partial(kernel, times, ring), out_shape=jax.Shap...  56.2 us
    unnamed x13, local copies, waits for them, and re-layouts  6.02 us

profile of v3, /device:TPU:4, one launch (start us, length us, event | category | flops | bytes accessed | tf_op | source)
XLA Modules:
  0.0 62.2 jit_solution(1271005780862012069)
XLA Ops:
  0.0 0.0 copy-start
  0.0 1.0 %copy-done = f32[1,1024,128]{2,1,0:T(8,128)S(1)} copy-done((f32[1,1024,128]{2,1,0:T(8,128)S(1)}, f32[1,1024,128]{2,1,0:T(8,128)}, u32[]{:S(2)}) %copy-start) | copy-done | bytes 524312
  1.0 0.0 copy-start.1
  1.0 1.0 %copy-done.1 = f32[6,128,128]{2,1,0:T(8,128)S(1)} copy-done((f32[6,128,128]{2,1,0:T(8,128)S(1)}, f32[6,128,128]{2,1,0:T(8,128)}, u32[]{:S(2)}) %copy-start.1) | copy-done | bytes 393240
  2.0 0.0 copy-start.2
  2.0 0.8 %copy-done.2 = f32[128,128]{1,0:T(8,128)S(1)} copy-done((f32[128,128]{1,0:T(8,128)S(1)}, f32[128,128]{1,0:T(8,128)}, u32[]{:S(2)}) %copy-start.2) | copy-done | bytes 65560
  2.9 0.0 copy-start.3
  2.9 0.8 %copy-done.3 = f32[128,128]{1,0:T(8,128)S(1)} copy-done((f32[128,128]{1,0:T(8,128)S(1)}, f32[128,128]{1,0:T(8,128)}, u32[]{:S(2)}) %copy-start.3) | copy-done | bytes 65560
  3.7 0.0 copy-start.4
  3.7 0.8 %copy-done.4 = s32[1024,6]{0,1:T(8,128)S(1)} copy-done((s32[1024,6]{0,1:T(8,128)S(1)}, s32[1024,6]{0,1:T(8,128)}, u32[]{:S(2)}) %copy-start.4) | copy-done | bytes 24600
  4.5 0.0 copy-start.5
  4.5 0.8 %copy-done.5 = s32[1024,6]{0,1:T(8,128)S(1)} copy-done((s32[1024,6]{0,1:T(8,128)S(1)}, s32[1024,6]{0,1:T(8,128)}, u32[]{:S(2)}) %copy-start.5) | copy-done | bytes 24600
  5.2 56.2 %shard_map.64 = f32[1,1024,128]{2,1,0:T(8,128)S(1)} custom-call(f32[1,1024,128]{2,1,0:T(8,128)S(1)} %copy-done, f32[128,128]{1,0:T(8,128)S(1)} %copy-done.2, f32[6,128,128]{2,1,0:T(8,128)S(1)} %copy-done.1, s32[6,1024]{1,0:T(8,128)S(1)} %bitcast.2, s32[6,1024]{1,0:T(8,128)S(1)} %bitcast.3, f32[128,128]{1,0:T(8,128)S(1)} %copy-done.3), custom_call_target="tpu_custom_call" | custom-call | tf_op jit(solution)/shard_map/pallas_call | solution.py:353
  61.4 0.8 %copy.8 = f32[1,1024,128]{2,1,0:T(8,128)} copy(f32[1,1024,128]{2,1,0:T(8,128)S(1)} %shard_map.64) | data formatting | bytes 1048576
Async XLA Ops:
  0.0 1.0 %copy-start = (f32[1,1024,128]{2,1,0:T(8,128)S(1)}, f32[1,1024,128]{2,1,0:T(8,128)}, u32[]{:S(2)}) copy-start(f32[1,1024,128]{2,1,0:T(8,128)} %starts.1) | copy-start | bytes 1572868
  1.0 1.0 %copy-start.1 = (f32[6,128,128]{2,1,0:T(8,128)S(1)}, f32[6,128,128]{2,1,0:T(8,128)}, u32[]{:S(2)}) copy-start(f32[6,128,128]{2,1,0:T(8,128)} %lifts.1) | copy-start | bytes 1179652
  2.0 0.8 %copy-start.2 = (f32[128,128]{1,0:T(8,128)S(1)}, f32[128,128]{1,0:T(8,128)}, u32[]{:S(2)}) copy-start(f32[128,128]{1,0:T(8,128)} %volume.1) | copy-start | bytes 196612
  2.9 0.8 %copy-start.3 = (f32[128,128]{1,0:T(8,128)S(1)}, f32[128,128]{1,0:T(8,128)}, u32[]{:S(2)}) copy-start(f32[128,128]{1,0:T(8,128)} %constant.2.clone.basis_t) | copy-start | bytes 196612
  3.7 0.8 %copy-start.4 = (s32[1024,6]{0,1:T(8,128)S(1)}, s32[1024,6]{0,1:T(8,128)}, u32[]{:S(2)}) copy-start(s32[1024,6]{0,1:T(8,128)} %param.9) | copy-start | bytes 73732
  4.5 0.8 %copy-start.5 = (s32[1024,6]{0,1:T(8,128)S(1)}, s32[1024,6]{0,1:T(8,128)}, u32[]{:S(2)}) copy-start(s32[1024,6]{0,1:T(8,128)} %param.10) | copy-start | bytes 73732
